TPU v7x, 512 devices: a whole 4x4x16 slice. The times are simulated.
512 devices in a mesh: ctx: 64 (over z, y), head: 8 (over x, core).
Axes of the slice: x: 4, y: 4, z: 16, core: 2. Of those that a mesh axis runs over, the one named last changes fastest.
Arguments:
- query_lin: bfloat16 [8192, 256], P('ctx', 'head'), may hold values from -4 to 4
- key_lin: bfloat16 [8192, 256], P('ctx', 'head'), may hold values from -4 to 4
- values: bfloat16 [8192, 2048], P('ctx', 'head'), may hold values from -24 to 24
- win_queries: bfloat16 [8192, 2048], P('ctx', 'head'), may hold values from -6 to 6
- win_keys: bfloat16 [8192, 2048], P('ctx', 'head'), may hold values from -6 to 6
- gain: float32 [2048], P('head'), may hold values from 0.1 to 1.9
- grad_out: bfloat16 [8192, 2048], P('ctx', 'head'), may hold values from -6 to 6
Outputs:
- mixed_out: bfloat16 [8192, 2048], P('ctx', 'head')
- grad_query_lin: bfloat16 [8192, 256], P('ctx', 'head')
- grad_key_lin: bfloat16 [8192, 256], P('ctx', 'head')
- grad_values: bfloat16 [8192, 2048], P('ctx', 'head')
- grad_win_queries: bfloat16 [8192, 2048], P('ctx', 'head')
- grad_win_keys: bfloat16 [8192, 2048], P('ctx', 'head')
All inputs are finite; a program needn't handle non-finite values.
Results may differ from a plain program's by a relative error of at most 0.015.
Values may be sent and summed in bfloat16 or wider, within the bound.
A program may use at most 128 MiB of HBM per device.

v0:
```python
import math
import jax
import jax.numpy as jnp
from jax import lax
from jax.sharding import PartitionSpec as P

HEADS = 16
KD = 16
DV = 128
WD = 128
WINDOW = 128
epsilon = 1e-06


def from_behind(value, axis, by):
    size = lax.axis_size(axis)
    pairs = [(i, i + by) for i in range(size) if 0 <= i + by < size]
    return lax.ppermute(value, axis, pairs)


def prefix_2(value, axis, join, neutral, backward):
    count = lax.axis_size(axis)
    place = lax.axis_index(axis)
    ahead = count - 1 - place if backward else place
    gathered = lax.all_gather(value.astype(jnp.bfloat16), axis)
    state = jnp.zeros_like(value) + jnp.asarray(neutral, value.dtype)

    def one(step, state):
        source = count - 1 - step if backward else step
        return join(state, lax.dynamic_index_in_dim(gathered, source, 0, False).astype(value.dtype))

    return lax.fori_loop(0, ahead, one, state)


def features_cols(points):
    head_count = points.shape[0]
    key_depth = points.shape[1]
    tok_count = points.shape[2]
    linear_part = points / math.sqrt(math.sqrt(key_depth))
    outer_part = (points[:, :, None, :] * points[:, None, :, :]).reshape(
        head_count, key_depth * key_depth, tok_count
    )
    outer_part = outer_part / (math.sqrt(2.0) * math.sqrt(key_depth))
    return jnp.concatenate([jnp.ones_like(points[:, :1, :]), linear_part, outer_part], axis=1)


def accumulate(earlier, upcoming):
    return earlier + upcoming


def window_math(query_blocks, key_pairs, value_pairs, dout_blocks, allowed, scale_win):
    scores = (
        jnp.einsum("bthe,bshe->bhts", query_blocks, key_pairs, preferred_element_type=jnp.float32)
        * scale_win
    )
    row_top = jnp.max(jnp.where(allowed, scores, -jnp.inf), axis=-1, keepdims=True)
    weights = jnp.where(allowed, jnp.exp(scores - row_top), 0.0)
    row_total = jnp.sum(weights, axis=-1, keepdims=True)
    soft_probs = weights / row_total
    probs_round = soft_probs.astype(jnp.bfloat16)
    win_out = jnp.einsum(
        "bhts,bshd->bthd", probs_round, value_pairs, preferred_element_type=jnp.float32
    )
    grad_prob = jnp.einsum(
        "bthd,bshd->bhts", dout_blocks, value_pairs, preferred_element_type=jnp.float32
    )
    row_delta = jnp.transpose(
        jnp.sum(dout_blocks.astype(jnp.float32) * win_out, axis=-1), (0, 2, 1)
    )[..., None]
    grad_score = (soft_probs * (grad_prob - row_delta)).astype(jnp.bfloat16)
    grad_query = (
        jnp.einsum("bhts,bshe->bthe", grad_score, key_pairs, preferred_element_type=jnp.float32)
        * scale_win
    )
    grad_keys = (
        jnp.einsum("bhts,bthe->bshe", grad_score, query_blocks, preferred_element_type=jnp.float32)
        * scale_win
    )
    grad_vals = jnp.einsum(
        "bhts,bthd->bshd", probs_round, dout_blocks, preferred_element_type=jnp.float32
    )
    return (win_out, grad_query, grad_keys, grad_vals, row_top, row_total, row_delta)


def shards(query_lin, key_lin, values, win_queries, win_keys, gain, grad_out):
    tok_rows = query_lin.shape[0]
    head_count = values.shape[1] // DV
    full_width = HEADS * DV
    scale_lin = 1.0 / math.sqrt(KD)
    scale_win = 1.0 / math.sqrt(WD)
    ctx_index = lax.axis_index("ctx")
    tail_start = tok_rows - WINDOW
    rim_keys, rim_values = from_behind((win_keys, values), "ctx", 1)
    query_h = query_lin.reshape(tok_rows, head_count, KD)
    key_h = key_lin.reshape(tok_rows, head_count, KD)
    value_h = values.reshape(tok_rows, head_count, DV)
    query_cols = jnp.transpose(query_h, (1, 2, 0)).astype(jnp.float32)
    key_cols = jnp.transpose(key_h, (1, 2, 0)).astype(jnp.float32)
    query_feat, pull_query = jax.vjp(features_cols, query_cols)
    key_feat, pull_key = jax.vjp(features_cols, key_cols)
    query_phi = query_feat.astype(jnp.bfloat16)
    key_phi = key_feat.astype(jnp.bfloat16)
    local_state = jnp.einsum("hfs,shd->hfd", key_phi, value_h, preferred_element_type=jnp.float32)
    state_zero = jnp.zeros_like(local_state)
    prefix = prefix_2(local_state, "ctx", accumulate, state_zero, False)
    prefix_round = prefix.astype(jnp.bfloat16)
    lin_score = (
        jnp.einsum("thk,shk->hts", query_h, key_h, preferred_element_type=jnp.float32) * scale_lin
    )
    causal = jnp.tril(jnp.ones((tok_rows, tok_rows), jnp.bool_))
    kernel = jnp.where(causal, 1.0 + lin_score + 0.5 * lin_score * lin_score, 0.0).astype(
        jnp.bfloat16
    )
    linear_out = jnp.einsum("hts,shd->thd", kernel, value_h, preferred_element_type=jnp.float32)
    linear_out = linear_out + jnp.einsum(
        "hft,hfd->thd", query_phi, prefix_round, preferred_element_type=jnp.float32
    )
    linear_flat = linear_out.reshape(tok_rows, head_count * DV)
    dout_f = grad_out.astype(jnp.float32)
    square_sum = lax.psum(jnp.sum(linear_flat * linear_flat, axis=1), "head")
    inverse = (1.0 / jnp.sqrt(square_sum / full_width + epsilon))[:, None]
    blocks = tok_rows // WINDOW
    keys_ext = jnp.concatenate([rim_keys, win_keys], axis=0).reshape(
        blocks + 1, WINDOW, head_count, WD
    )
    values_ext = jnp.concatenate([rim_values, values], axis=0).reshape(
        blocks + 1, WINDOW, head_count, DV
    )
    key_pairs = jnp.concatenate([keys_ext[:-1], keys_ext[1:]], axis=1)
    value_pairs = jnp.concatenate([values_ext[:-1], values_ext[1:]], axis=1)
    query_blocks = win_queries.reshape(blocks, WINDOW, head_count, WD)
    dout_blocks = grad_out.reshape(blocks, WINDOW, head_count, DV)
    row_pos = jnp.arange(WINDOW, dtype=jnp.int32)[:, None]
    col_pos = jnp.arange(2 * WINDOW, dtype=jnp.int32)[None, :]
    band_mask = (col_pos > row_pos) & (col_pos <= row_pos + WINDOW)
    key_start = (
        ctx_index * tok_rows
        + jnp.arange(blocks, dtype=jnp.int32)[:, None, None] * WINDOW
        - WINDOW
        + col_pos[None]
    )
    allowed = (band_mask[None] & (key_start >= 0))[:, None]
    win_out, grad_wq, key_grads, value_grads, row_top, row_total, row_delta = window_math(
        query_blocks, key_pairs, value_pairs, dout_blocks, allowed, scale_win
    )
    window_flat = win_out.reshape(tok_rows, head_count * DV)
    mixed_out = (linear_flat * inverse * gain + window_flat).astype(jnp.bfloat16)
    cross_sum = lax.psum(jnp.sum(gain * dout_f * linear_flat, axis=1), "head")
    grad_lin = (
        inverse * gain * dout_f
        - linear_flat * inverse * inverse * inverse * (cross_sum / full_width)[:, None]
    ).astype(jnp.bfloat16)
    grad_lin_h = grad_lin.reshape(tok_rows, head_count, DV)
    value_dot = jnp.einsum("thd,shd->hts", grad_lin_h, value_h, preferred_element_type=jnp.float32)
    grad_score = jnp.where(causal, value_dot * (1.0 + lin_score), 0.0).astype(jnp.bfloat16)
    query_pull = jnp.einsum(
        "thd,hfd->hft", grad_lin_h, prefix_round, preferred_element_type=jnp.float32
    )
    grad_query = (
        jnp.einsum("hts,shk->thk", grad_score, key_h, preferred_element_type=jnp.float32)
        * scale_lin
    )
    grad_query = grad_query + jnp.transpose(pull_query(query_pull)[0], (2, 0, 1))
    local_back = jnp.einsum(
        "hft,thd->hfd", query_phi, grad_lin_h, preferred_element_type=jnp.float32
    )
    suffix = prefix_2(local_back, "ctx", accumulate, state_zero, True)
    suffix_round = suffix.astype(jnp.bfloat16)
    grad_value_lin = jnp.einsum(
        "hts,thd->shd", kernel, grad_lin_h, preferred_element_type=jnp.float32
    )
    grad_value_lin = grad_value_lin + jnp.einsum(
        "hfs,hfd->shd", key_phi, suffix_round, preferred_element_type=jnp.float32
    )
    key_pull = jnp.einsum("shd,hfd->hfs", value_h, suffix_round, preferred_element_type=jnp.float32)
    grad_key = (
        jnp.einsum("hts,thk->shk", grad_score, query_h, preferred_element_type=jnp.float32)
        * scale_lin
    )
    grad_key = grad_key + jnp.transpose(pull_key(key_pull)[0], (2, 0, 1))
    pad_tail = ((0, 1), (0, 0), (0, 0), (0, 0))
    pad_head = ((1, 0), (0, 0), (0, 0), (0, 0))
    key_ext_grad = jnp.pad(key_grads[:, :WINDOW], pad_tail) + jnp.pad(
        key_grads[:, WINDOW:], pad_head
    )
    value_ext_grad = jnp.pad(value_grads[:, :WINDOW], pad_tail) + jnp.pad(
        value_grads[:, WINDOW:], pad_head
    )
    key_own = key_ext_grad[1:].reshape(tok_rows, head_count * WD)
    value_own = value_ext_grad[1:].reshape(tok_rows, head_count * DV)
    back_keys, back_values = (
        from_behind(
            key_ext_grad[0].reshape(WINDOW, head_count * WD).astype(jnp.bfloat16), "ctx", -1
        ).astype(jnp.float32),
        from_behind(
            value_ext_grad[0].reshape(WINDOW, head_count * DV).astype(jnp.bfloat16), "ctx", -1
        ).astype(jnp.float32),
    )
    key_own = jnp.concatenate([key_own[:tail_start], key_own + back_keys], axis=0)
    value_own = jnp.concatenate([value_own[:tail_start], value_own + back_values], axis=0)
    grad_query_lin = grad_query.astype(jnp.bfloat16).reshape(tok_rows, head_count * KD)
    grad_key_lin = grad_key.astype(jnp.bfloat16).reshape(tok_rows, head_count * KD)
    grad_values = (grad_value_lin.reshape(tok_rows, head_count * DV) + value_own).astype(
        jnp.bfloat16
    )
    grad_win_queries = grad_wq.reshape(tok_rows, head_count * WD).astype(jnp.bfloat16)
    grad_win_keys = key_own.astype(jnp.bfloat16)
    return (mixed_out, grad_query_lin, grad_key_lin, grad_values, grad_win_queries, grad_win_keys)


def solution(mesh):
    placed = (
        P("ctx", "head"),
        P("ctx", "head"),
        P("ctx", "head"),
        P("ctx", "head"),
        P("ctx", "head"),
        P("head"),
        P("ctx", "head"),
    )
    return jax.shard_map(
        shards,
        mesh=mesh,
        in_specs=placed,
        out_specs=(
            P("ctx", "head"),
            P("ctx", "head"),
            P("ctx", "head"),
            P("ctx", "head"),
            P("ctx", "head"),
            P("ctx", "head"),
        ),
        check_vma=False,
    )
```

profile of v0, /device:TPU:2, one launch (start us, length us, event | category | flops | bytes accessed | tf_op | source)
XLA Modules:
  0.0 470.7 jit_solution(8082545731358047730)
XLA Ops:
  8.7 1.8 convolution_convert_fusion.1
  10.6 3.5 collective-permute-start
  15.0 3.5 collective-permute-start.1
  19.6 1.0 copy.121
  25.0 150.1 %all-gather.5.cloned.1.call-done = bf16[128,273,128]{2,1,0:T(8,128)(2,1)} async-done(((bf16[2,273,128]{2,1,0:T(8,128)(2,1)}), bf16[128,273,128]{2,1,0:T(8,128)(2,1)}) %all-gather.5.cloned.1.call-update) | async-done | bytes 8945680 | tf_op jit(solution)/shard_map/all_gather | solution.py:25
  176.0 10.0 %all-reduce.4 = (f32[128]{0:T(128)S(1)}, f32[128]{0:T(128)S(1)}) all-reduce(f32[128]{0:T(128)S(1)} %get-tuple-element.137, f32[128]{0:T(128)S(1)} %multiply_reduce_fusion.4), channel_id=1, replica_groups=mesh['ctx'=64,'head'=8] {'head'}, use_global_device_ids=true, to_apply=%region_3.4 | all-reduce | flops 256 | bytes 2048 | tf_op jit(solution)/shard_map/psum | solution.py:120
  186.9 1.0 convolution_convert_fusion
  189.5 1.3 collective-permute-start.3
  191.3 1.3 collective-permute-start.2
  192.7 2.9 collective-permute-done.3
  197.7 202.1 %all-gather.7.cloned.1.call-done = bf16[128,273,128]{2,1,0:T(8,128)(2,1)} async-done(((bf16[2,273,128]{2,1,0:T(8,128)(2,1)}), bf16[128,273,128]{2,1,0:T(8,128)(2,1)}) %all-gather.7.cloned.1.call-update) | async-done | bytes 8945680 | tf_op jit(solution)/shard_map/all_gather | solution.py:25
  399.9 61.5 %while.23 = (s32[]{:T(128)}, f32[2,273,128]{2,1,0:T(8,128)S(1)}, s32[]{:T(128)}, bf16[64,2,273,128]{3,2,1,0:T(8,128)(2,1)}, s32[]{:T(128)}, /*index=5*/s32[]{:T(128)}, s32[]{:T(128)}, s32[]{:T(128)}) while((s32[]{:T(128)}, f32[2,273,128]{2,1,0:T(8,128)S(1)}, s32[]{:T(128)}, bf16[64,2,273,128]{3,2,1,0:T(8,128)(2,1)}, s32[]{:T(128)}, ...), condition=%wide.region_11.12_spmd, body=%wide.region_10.11_spmd.sunk | while | flops 139782 | bytes 699023 | solution.py:32
  399.9 1.0 convert_add_fusion.5
  400.9 1.0 convert_add_fusion.5
  401.9 1.0 convert_add_fusion.5
  402.8 1.0 convert_add_fusion.5
  403.8 1.0 convert_add_fusion.5
  404.8 1.0 convert_add_fusion.5
  405.8 1.0 convert_add_fusion.5
  406.7 1.0 convert_add_fusion.5
  407.7 1.0 convert_add_fusion.5
  408.7 1.0 convert_add_fusion.5
  409.7 1.0 convert_add_fusion.5
  410.6 1.0 convert_add_fusion.5
  411.6 1.0 convert_add_fusion.5
  412.6 1.0 convert_add_fusion.5
  413.6 1.0 convert_add_fusion.5
  414.6 1.0 convert_add_fusion.5
  415.5 1.0 convert_add_fusion.5
  416.5 1.0 convert_add_fusion.5
  417.5 1.0 convert_add_fusion.5
  418.5 1.0 convert_add_fusion.5
  419.4 1.0 convert_add_fusion.5
  420.4 1.0 convert_add_fusion.5
  421.4 1.0 convert_add_fusion.5
  422.4 1.0 convert_add_fusion.5
  423.3 1.0 convert_add_fusion.5
  424.3 1.0 convert_add_fusion.5
  425.3 1.0 convert_add_fusion.5
  426.3 1.0 convert_add_fusion.5
  427.3 1.0 convert_add_fusion.5
  428.2 1.0 convert_add_fusion.5
  429.2 1.0 convert_add_fusion.5
  430.2 1.0 convert_add_fusion.5
  431.2 1.0 convert_add_fusion.5
  432.1 1.0 convert_add_fusion.5
  433.1 1.0 convert_add_fusion.5
  434.1 1.0 convert_add_fusion.5
  435.1 1.0 convert_add_fusion.5
  436.0 1.0 convert_add_fusion.5
  437.0 1.0 convert_add_fusion.5
  438.0 1.0 convert_add_fusion.5
  440.9 1.0 convert_add_fusion.5
  441.9 1.0 convert_add_fusion.5
  442.9 1.0 convert_add_fusion.5
  443.9 1.0 convert_add_fusion.5
  444.8 1.0 convert_add_fusion.5
  449.7 1.0 convert_add_fusion.5
  450.7 1.0 convert_add_fusion.5
  451.7 1.0 convert_add_fusion.5
  452.7 1.0 convert_add_fusion.5
  453.6 1.0 convert_add_fusion.5
  459.5 1.0 convert_add_fusion.5
  460.5 1.0 convert_add_fusion.5
  (88 shorter events, 26.8 us)
Async XLA Ops:
  7.2 168.3 %copy-start = (bf16[128,256]{1,0:T(8,128)(2,1)S(1)}, bf16[128,256]{1,0:T(8,128)(2,1)}, u32[]{:S(2)}) copy-start(bf16[128,256]{1,0:T(8,128)(2,1)} %param.13) | copy-start | bytes 196612
  7.2 168.7 %copy-start.1 = (bf16[128,256]{1,0:T(8,128)(2,1)S(1)}, bf16[128,256]{1,0:T(8,128)(2,1)}, u32[]{:S(2)}) copy-start(bf16[128,256]{1,0:T(8,128)(2,1)} %param.17) | copy-start | bytes 196612
  7.2 168.7 %copy-start.4 = (f32[256]{0:T(256)S(1)}, f32[256]{0:T(256)}, u32[]{:S(2)}) copy-start(f32[256]{0:T(256)} %param.16) | copy-start | bytes 3076
  7.2 167.9 %all-gather.5.cloned.1.call-start = ((), (), s32[]{:S(2)}) async-start(), calls=%async_computation | async-start | bytes 9318400 | tf_op jit(solution)/shard_map/all_gather | solution.py:25
  10.5 389.3 %all-gather.7.cloned.1.call-start = ((), (), s32[]{:S(2)}) async-start(), calls=%async_computation.1 | async-start | bytes 9318400 | tf_op jit(solution)/shard_map/all_gather | solution.py:25
  10.6 13.6 %collective-permute-start = (bf16[128,256]{1,0:T(8,128)(2,1)}, bf16[128,256]{1,0:T(8,128)(2,1)S(1)}, u32[]{:S(2)}, u32[]{:S(2)}) collective-permute-start(bf16[128,256]{1,0:T(8,128)(2,1)} %param.13), channel_id=1, source_target_pairs={{0,8},{8,16},{16,24},{24,32},{32,40},{40,48},{48,56},{56,64},{64,7... | collective-permute-start | bytes 196616 | tf_op jit(solution)/shard_map/ppermute | solution.py:18
  15.0 9.0 %collective-permute-start.1 = (bf16[128,256]{0,1:T(8,128)(2,1)S(1)}, bf16[128,256]{0,1:T(8,128)(2,1)S(1)}, u32[]{:S(2)}, u32[]{:S(2)}) collective-permute-start(bf16[128,256]{0,1:T(8,128)(2,1)S(1)} %copy.83), channel_id=1, source_target_pairs={{0,8},{8,16},{16,24},{24,32},{32,40},{40,48},{48,56},{56,64},{64,7... | collective-permute-start | bytes 196616 | tf_op jit(solution)/shard_map/ppermute | solution.py:18
  24.3 172.7 %copy-start.2 = (bf16[128,32]{0,1:T(8,128)(2,1)S(1)}, bf16[128,32]{0,1:T(8,128)(2,1)}, u32[]{:S(2)}) copy-start(bf16[128,32]{0,1:T(8,128)(2,1)} %param.12) | copy-start | bytes 24580
  175.1 287.2 %copy-start.3 = (bf16[128,32]{0,1:T(8,128)(2,1)S(1)}, bf16[128,32]{0,1:T(8,128)(2,1)}, u32[]{:S(2)}) copy-start(bf16[128,32]{0,1:T(8,128)(2,1)} %param.11) | copy-start | bytes 24580
  189.5 6.2 %collective-permute-start.3 = (bf16[128,256]{0,1:T(8,128)(2,1)S(1)}, bf16[128,256]{0,1:T(8,128)(2,1)S(1)}, u32[]{:S(2)}, u32[]{:S(2)}) collective-permute-start(bf16[128,256]{0,1:T(8,128)(2,1)S(1)} %bitcast.205), channel_id=1, source_target_pairs={{8,0},{16,8},{24,16},{32,24},{40,32},{48,40},{56,48},{64,56},{72,6... | collective-permute-start | bytes 196616 | tf_op jit(solution)/shard_map/ppermute | solution.py:18
  191.3 271.9 %collective-permute-start.2 = (bf16[128,256]{1,0:T(8,128)(2,1)S(1)}, bf16[128,256]{1,0:T(8,128)(2,1)S(1)}, u32[]{:S(2)}, u32[]{:S(2)}) collective-permute-start(bf16[128,256]{1,0:T(8,128)(2,1)S(1)} %copy.99), channel_id=1, source_target_pairs={{8,0},{16,8},{24,16},{32,24},{40,32},{48,40},{56,48},{64,56},{72,6... | collective-permute-start | bytes 196616 | tf_op jit(solution)/shard_map/ppermute | solution.py:18
Sparse Core Ops, SparseCore 0:
  11.0 164.0 all-gather.4
  188.0 211.8 all-gather.6
where the time goes:
time: 473 us; the launch traced here: 471 us
  waiting for transfers between devices  355 us (75%)
  other arithmetic  65.1 us (14%)
  between operations  14.5 us (3%)
  blocking collectives  10 us (2%)
  starting transfers between devices  9.63 us (2%)
  matrix products  8.27 us (2%)
  local copies, waits for them, and re-layouts  6.56 us (1%)
    all_gather x2, waiting for transfers between devices, prefix_2(): gathered = lax.all_gather(value.astype(jnp.bfloat16), axis)  352 us
    add x63, other arithmetic, accumulate(): return earlier + upcoming  60.1 us
    psum x1, blocking collectives, shards(): square_sum = lax.psum(jnp.sum(linear_flat * linear_flat, axis=1), 'head')  10 us
    ppermute x4, starting transfers between devices, from_behind(): return lax.ppermute(value, axis, pairs)  9.55 us
  transfers between devices with their start and end apart: 6, of which 3 were waited for; matrix products, arithmetic and copies ran while one was open for 16% of the time, Pallas kernels for 0%

commit v1 on v0

--- a/solution.py
+++ b/solution.py
@@ -117,7 +117,7 @@
     )
     linear_flat = linear_out.reshape(tok_rows, head_count * DV)
     dout_f = grad_out.astype(jnp.float32)
-    square_sum = lax.psum(jnp.sum(linear_flat * linear_flat, axis=1), "head")
+    square_sum = jnp.sum(lax.all_gather(jnp.sum(linear_flat * linear_flat, axis=1), "head"), axis=0)
     inverse = (1.0 / jnp.sqrt(square_sum / full_width + epsilon))[:, None]
     blocks = tok_rows // WINDOW
     keys_ext = jnp.concatenate([rim_keys, win_keys], axis=0).reshape(

time: 473 us -> 482 us (1.019)
  blocking collectives: 10 us -> 20.7 us
    all_gather x0 -> x1, blocking collectives: none -> 10.7 us  [shards(): lax.all_gather(jnp.sum(linear_flat * linear_flat, axis=1), 'head')]
  transfers between devices with their start and end apart: 6 -> 6, of which waited for: 3 -> 3; matrix products, arithmetic and copies ran while one was open for 16% -> 15% of each run, Pallas kernels for 0% -> 0%
where the time goes in v1:
time: 482 us; the launch traced here: 480 us
  waiting for transfers between devices  353 us (73%)
  other arithmetic  65.1 us (14%)
  blocking collectives  20.7 us (4%)
  between operations  14.5 us (3%)
  starting transfers between devices  9.63 us (2%)
  matrix products  8.27 us (2%)
  local copies, waits for them, and re-layouts  6.56 us (1%)
    all_gather x2, waiting for transfers between devices, prefix_2(): gathered = lax.all_gather(value.astype(jnp.bfloat16), axis)  350 us
    add x63, other arithmetic, accumulate(): return earlier + upcoming  60.1 us
    all_gather x1, blocking collectives, shards(): lax.all_gather(jnp.sum(linear_flat * linear_flat, axis=1), 'head')  10.7 us
    psum x1, blocking collectives, shards(): cross_sum = lax.psum(jnp.sum(gain * dout_f * linear_flat, axis=1), 'head')  10 us
  transfers between devices with their start and end apart: 6, of which 3 were waited for; matrix products, arithmetic and copies ran while one was open for 15% of the time, Pallas kernels for 0%

profile of v1, /device:TPU:2, one launch (start us, length us, event | category | flops | bytes accessed | tf_op | source)
XLA Modules:
  0.0 479.6 jit_solution(8096287302822193234)
XLA Ops:
  8.7 1.8 convolution_convert_fusion.1
  10.6 3.5 collective-permute-start
  15.0 3.5 collective-permute-start.1
  19.6 1.0 copy.121
  25.0 150.1 %all-gather.7.cloned.1.call-done = bf16[128,273,128]{2,1,0:T(8,128)(2,1)} async-done(((bf16[2,273,128]{2,1,0:T(8,128)(2,1)}), bf16[128,273,128]{2,1,0:T(8,128)(2,1)}) %all-gather.7.cloned.1.call-update) | async-done | bytes 8945680 | tf_op jit(solution)/shard_map/all_gather | solution.py:25
  176.0 10.0 %psum.7 = f32[128]{0:T(128)S(1)} all-reduce(f32[128]{0:T(128)S(1)} %multiply_reduce_fusion.4), channel_id=1, replica_groups=mesh['ctx'=64,'head'=8] {'head'}, use_global_device_ids=true, to_apply=%region_7.8 | all-reduce | flops 128 | bytes 1024 | tf_op jit(solution)/shard_map/psum | solution.py:148
  186.0 10.7 %all-gather.3 = f32[8,1,128]{2,1,0:T(1,128)S(1)} all-gather(f32[1,1,128]{2,1,0:T(1,128)S(1)} %bitcast.212), channel_id=3, replica_groups=mesh['ctx'=64,'head'=8] {'head'}, dimensions={0}, use_global_device_ids=true | all-gather | bytes 4608 | tf_op jit(solution)/shard_map/all_gather | solution.py:120
  197.6 1.0 convolution_convert_fusion
  200.2 1.3 collective-permute-start.3
  202.0 1.3 collective-permute-start.2
  203.4 2.9 collective-permute-done.3
  208.5 200.3 %all-gather.9.cloned.1.call-done = bf16[128,273,128]{2,1,0:T(8,128)(2,1)} async-done(((bf16[2,273,128]{2,1,0:T(8,128)(2,1)}), bf16[128,273,128]{2,1,0:T(8,128)(2,1)}) %all-gather.9.cloned.1.call-update) | async-done | bytes 8945680 | tf_op jit(solution)/shard_map/all_gather | solution.py:25
  408.8 61.5 %while.23 = (s32[]{:T(128)}, f32[2,273,128]{2,1,0:T(8,128)S(1)}, s32[]{:T(128)}, bf16[64,2,273,128]{3,2,1,0:T(8,128)(2,1)}, s32[]{:T(128)}, /*index=5*/s32[]{:T(128)}, s32[]{:T(128)}, s32[]{:T(128)}) while((s32[]{:T(128)}, f32[2,273,128]{2,1,0:T(8,128)S(1)}, s32[]{:T(128)}, bf16[64,2,273,128]{3,2,1,0:T(8,128)(2,1)}, s32[]{:T(128)}, ...), condition=%wide.region_11.12_spmd, body=%wide.region_10.11_spmd.sunk | while | flops 139782 | bytes 699023 | solution.py:32
  408.9 1.0 convert_add_fusion.5
  409.8 1.0 convert_add_fusion.5
  410.8 1.0 convert_add_fusion.5
  411.8 1.0 convert_add_fusion.5
  412.8 1.0 convert_add_fusion.5
  413.8 1.0 convert_add_fusion.5
  414.7 1.0 convert_add_fusion.5
  415.7 1.0 convert_add_fusion.5
  416.7 1.0 convert_add_fusion.5
  417.7 1.0 convert_add_fusion.5
  418.6 1.0 convert_add_fusion.5
  419.6 1.0 convert_add_fusion.5
  420.6 1.0 convert_add_fusion.5
  421.6 1.0 convert_add_fusion.5
  422.5 1.0 convert_add_fusion.5
  423.5 1.0 convert_add_fusion.5
  424.5 1.0 convert_add_fusion.5
  425.5 1.0 convert_add_fusion.5
  426.5 1.0 convert_add_fusion.5
  427.4 1.0 convert_add_fusion.5
  428.4 1.0 convert_add_fusion.5
  429.4 1.0 convert_add_fusion.5
  430.4 1.0 convert_add_fusion.5
  431.3 1.0 convert_add_fusion.5
  432.3 1.0 convert_add_fusion.5
  433.3 1.0 convert_add_fusion.5
  434.3 1.0 convert_add_fusion.5
  435.2 1.0 convert_add_fusion.5
  436.2 1.0 convert_add_fusion.5
  437.2 1.0 convert_add_fusion.5
  438.2 1.0 convert_add_fusion.5
  439.2 1.0 convert_add_fusion.5
  440.1 1.0 convert_add_fusion.5
  441.1 1.0 convert_add_fusion.5
  442.1 1.0 convert_add_fusion.5
  443.1 1.0 convert_add_fusion.5
  444.0 1.0 convert_add_fusion.5
  445.0 1.0 convert_add_fusion.5
  448.9 1.0 convert_add_fusion.5
  449.9 1.0 convert_add_fusion.5
  450.9 1.0 convert_add_fusion.5
  451.9 1.0 convert_add_fusion.5
  452.8 1.0 convert_add_fusion.5
  458.7 1.0 convert_add_fusion.5
  459.7 1.0 convert_add_fusion.5
  460.6 1.0 convert_add_fusion.5
  461.6 1.0 convert_add_fusion.5
  462.6 1.0 convert_add_fusion.5
  467.5 1.0 convert_add_fusion.5
  468.5 1.0 convert_add_fusion.5
  469.4 1.0 convert_add_fusion.5
  (91 shorter events, 27.7 us)
Async XLA Ops:
  7.2 168.3 %copy-start = (bf16[128,256]{1,0:T(8,128)(2,1)S(1)}, bf16[128,256]{1,0:T(8,128)(2,1)}, u32[]{:S(2)}) copy-start(bf16[128,256]{1,0:T(8,128)(2,1)} %param.13) | copy-start | bytes 196612
  7.2 168.7 %copy-start.1 = (bf16[128,256]{1,0:T(8,128)(2,1)S(1)}, bf16[128,256]{1,0:T(8,128)(2,1)}, u32[]{:S(2)}) copy-start(bf16[128,256]{1,0:T(8,128)(2,1)} %param.17) | copy-start | bytes 196612
  7.2 168.7 %copy-start.4 = (f32[256]{0:T(256)S(1)}, f32[256]{0:T(256)}, u32[]{:S(2)}) copy-start(f32[256]{0:T(256)} %param.16) | copy-start | bytes 3076
  7.2 167.9 %all-gather.7.cloned.1.call-start = ((), (), s32[]{:S(2)}) async-start(), calls=%async_computation | async-start | bytes 9318400 | tf_op jit(solution)/shard_map/all_gather | solution.py:25
  10.5 398.3 %all-gather.9.cloned.1.call-start = ((), (), s32[]{:S(2)}) async-start(), calls=%async_computation.1 | async-start | bytes 9318400 | tf_op jit(solution)/shard_map/all_gather | solution.py:25
  10.6 13.6 %collective-permute-start = (bf16[128,256]{1,0:T(8,128)(2,1)}, bf16[128,256]{1,0:T(8,128)(2,1)S(1)}, u32[]{:S(2)}, u32[]{:S(2)}) collective-permute-start(bf16[128,256]{1,0:T(8,128)(2,1)} %param.13), channel_id=1, source_target_pairs={{0,8},{8,16},{16,24},{24,32},{32,40},{40,48},{48,56},{56,64},{64,7... | collective-permute-start | bytes 196616 | tf_op jit(solution)/shard_map/ppermute | solution.py:18
  15.0 9.0 %collective-permute-start.1 = (bf16[128,256]{0,1:T(8,128)(2,1)S(1)}, bf16[128,256]{0,1:T(8,128)(2,1)S(1)}, u32[]{:S(2)}, u32[]{:S(2)}) collective-permute-start(bf16[128,256]{0,1:T(8,128)(2,1)S(1)} %copy.83), channel_id=1, source_target_pairs={{0,8},{8,16},{16,24},{24,32},{32,40},{40,48},{48,56},{56,64},{64,7... | collective-permute-start | bytes 196616 | tf_op jit(solution)/shard_map/ppermute | solution.py:18
  24.3 183.4 %copy-start.2 = (bf16[128,32]{0,1:T(8,128)(2,1)S(1)}, bf16[128,32]{0,1:T(8,128)(2,1)}, u32[]{:S(2)}) copy-start(bf16[128,32]{0,1:T(8,128)(2,1)} %param.12) | copy-start | bytes 24580
  175.1 296.1 %copy-start.3 = (bf16[128,32]{0,1:T(8,128)(2,1)S(1)}, bf16[128,32]{0,1:T(8,128)(2,1)}, u32[]{:S(2)}) copy-start(bf16[128,32]{0,1:T(8,128)(2,1)} %param.11) | copy-start | bytes 24580
  200.2 6.2 %collective-permute-start.3 = (bf16[128,256]{0,1:T(8,128)(2,1)S(1)}, bf16[128,256]{0,1:T(8,128)(2,1)S(1)}, u32[]{:S(2)}, u32[]{:S(2)}) collective-permute-start(bf16[128,256]{0,1:T(8,128)(2,1)S(1)} %bitcast.206), channel_id=1, source_target_pairs={{8,0},{16,8},{24,16},{32,24},{40,32},{48,40},{56,48},{64,56},{72,6... | collective-permute-start | bytes 196616 | tf_op jit(solution)/shard_map/ppermute | solution.py:18
  202.0 270.1 %collective-permute-start.2 = (bf16[128,256]{1,0:T(8,128)(2,1)S(1)}, bf16[128,256]{1,0:T(8,128)(2,1)S(1)}, u32[]{:S(2)}, u32[]{:S(2)}) collective-permute-start(bf16[128,256]{1,0:T(8,128)(2,1)S(1)} %copy.99), channel_id=1, source_target_pairs={{8,0},{16,8},{24,16},{32,24},{40,32},{48,40},{56,48},{64,56},{72,6... | collective-permute-start | bytes 196616 | tf_op jit(solution)/shard_map/ppermute | solution.py:18
Sparse Core Ops, SparseCore 0:
  11.0 164.0 all-gather.6
  198.7 210.0 all-gather.8
